TPU v7x, 256 devices: a whole 4x4x8 slice. The times are simulated.
256 devices in a mesh: ray: 16 (over y, z_lo), pix: 16 (over z_hi, x, core).
Axes of the slice: x: 4, y: 4, z: 8 (z_hi: 2, z_lo: 4; z = z_hi * 4 + z_lo), core: 2. Of those that a mesh axis runs over, the one named last changes fastest.
Arguments:
- positions: float32 [2, 16384], P(None, 'ray'), may hold values from -2 to 2
- directions: float32 [2, 16384], P(None, 'ray'), may hold values from -0.35 to 0.35
- path: float32 [16384], P('ray'), may hold values from -9 to 9
- amplitude: float32 [16384], P('ray'), may hold values from 0.3 to 3
- psf_grad: float32 [3, 1024, 1024], P(None, 'pix', 'ray'), may hold values from -0.3 to 0.3
Outputs:
- psf: float32 [3, 1024, 1024], P(None, 'pix', 'ray')
- ray_grad: float32 [6, 16384], P(None, 'ray')
All inputs are finite; a program needn't handle non-finite values.
Results may differ from a plain program's by a relative error of at most 0.0054.
Values may be sent and summed in bfloat16 or wider, within the bound.
A program may use at most 192 MiB of HBM per device.

v0:
```python
import math
import jax
import jax.numpy as jnp
from jax import lax
from jax.sharding import PartitionSpec as P

NPIX = 1024
wave_scales = (1.2088, 1.0, 0.8953)
two_pi = 2.0 * math.pi


def centred(start, count):
    return (start + jnp.arange(count)).astype(jnp.float32) - 0.5 * NPIX + 0.5


def build_tables(rays, rows_x, cols_y, norm):
    row_list = []
    col_list = []
    weight = (rays[5] * norm)[:, None]
    for wave in range(3):
        scale = wave_scales[wave]
        angle = scale * (
            rays[4][:, None]
            + two_pi
            * (
                rays[2][:, None] * (rows_x[None, :] - rays[0][:, None])
                - rays[3][:, None] * rays[1][:, None]
            )
        )
        row_list.append(jnp.stack([weight * jnp.cos(angle), weight * jnp.sin(angle)]))
        beta = scale * two_pi * cols_y[:, None] * rays[3][None, :]
        col_list.append(jnp.stack([jnp.cos(beta), jnp.sin(beta)]))
    return (jnp.stack(row_list), jnp.stack(col_list))


def mixing(a_re, a_im):
    upper = jnp.concatenate([a_re, a_im], axis=1)
    lower = jnp.concatenate([-a_im, a_re], axis=1)
    return jnp.concatenate([upper, lower], axis=0).astype(jnp.bfloat16)


def product(left, right, dims):
    return lax.dot_general(left, right, dims, preferred_element_type=jnp.float32)


def block_count(count):
    return max(1, min(16, count // 256))


def field_terms(row_tab, col_tab):
    count = row_tab.shape[2]
    nblk = block_count(count)
    blk = count // nblk

    def step(index, total):
        a_blk = lax.dynamic_slice_in_dim(row_tab, index * blk, blk, 2)
        b_blk = lax.dynamic_slice_in_dim(col_tab, index * blk, blk, 3)
        parts = []
        for wave in range(3):
            left = jnp.concatenate([b_blk[wave, 0], b_blk[wave, 1]], axis=1).astype(jnp.bfloat16)
            parts.append(
                product(left, mixing(a_blk[wave, 0], a_blk[wave, 1]), (((1,), (0,)), ((), ())))
            )
        return total + jnp.concatenate(parts, axis=1)

    init = jnp.zeros((col_tab.shape[2], 6 * row_tab.shape[3]), jnp.float32)
    return lax.fori_loop(0, nblk, step, init)


def ray_partials(row_tab, col_tab, rows_x, cols_y, cotangent):
    count = row_tab.shape[2]
    nblk = block_count(count)
    blk = count // nblk
    plen = rows_x.shape[0]

    def one_block(index):
        a_blk = lax.dynamic_slice_in_dim(row_tab, index * blk, blk, 2)
        b_blk = lax.dynamic_slice_in_dim(col_tab, index * blk, blk, 3)
        first = jnp.zeros((blk,), jnp.float32)
        second = jnp.zeros((blk,), jnp.float32)
        third = jnp.zeros((blk,), jnp.float32)
        fourth = jnp.zeros((blk,), jnp.float32)
        for wave in range(3):
            scale = wave_scales[wave]
            a_re = a_blk[wave, 0]
            a_im = a_blk[wave, 1]
            b_re = b_blk[wave, 0]
            b_im = b_blk[wave, 1]
            left = jnp.concatenate([b_re, b_im], axis=1).astype(jnp.bfloat16)
            mix = mixing(a_re, a_im)
            grad_u = cotangent[:, 2 * plen * wave : 2 * plen * (wave + 1)]
            proj = product(left, grad_u, (((0,), (0,)), ((), ())))
            d_are = proj[:blk, :plen] + proj[blk:, plen:]
            d_aim = proj[:blk, plen:] - proj[blk:, :plen]
            d_b = product(grad_u, mix, (((1,), (1,)), ((), ())))
            d_beta = d_b[:, blk:] * b_re - d_b[:, :blk] * b_im
            d_alpha = d_aim * a_re - d_are * a_im
            first = first + scale * jnp.sum(d_alpha, axis=1)
            second = second + scale * two_pi * jnp.sum(d_alpha * rows_x[None, :], axis=1)
            third = third + scale * two_pi * jnp.sum(d_beta * cols_y[:, None], axis=0)
            fourth = fourth + jnp.sum(d_are * a_re + d_aim * a_im, axis=1)
        return jnp.stack([first, second, third, fourth])

    out = lax.map(one_block, jnp.arange(nblk))
    return jnp.transpose(out, (1, 0, 2)).reshape(4, count)


def finish(sums, rays):
    return jnp.stack(
        [
            sums[0],
            -two_pi * rays[2] * sums[0],
            -two_pi * rays[3] * sums[0],
            (sums[1] - two_pi * rays[0] * sums[0]) / NPIX,
            (sums[2] - two_pi * rays[1] * sums[0]) / NPIX,
            sums[3] / rays[5],
        ]
    )


def intensity(field, psf_grad, clen, plen):
    shaped = field.reshape(clen, 3, 2, plen)
    psf = jnp.transpose(shaped[:, :, 0] ** 2 + shaped[:, :, 1] ** 2, (1, 2, 0))
    weight = jnp.transpose(psf_grad, (2, 0, 1))
    grad_u = (2.0 * weight[:, :, None, :] * shaped).reshape(clen, 6 * plen).astype(jnp.bfloat16)
    return (psf, grad_u)


def on_device(positions, directions, path, amplitude, psf_grad):
    rays = jnp.concatenate([positions, directions, path[None], amplitude[None]], axis=0)
    local = rays.shape[1]
    plen = NPIX // lax.axis_size("pix")
    clen = NPIX // lax.axis_size("ray")
    norm = 1.0 / math.sqrt(local * lax.axis_size("ray"))
    rows_x = centred(lax.axis_index("pix") * plen, plen)
    all_cols = centred(0, NPIX)
    row_tab, col_tab = build_tables(rays, rows_x, all_cols, norm)
    field = lax.psum_scatter(field_terms(row_tab, col_tab), "ray", scatter_dimension=0, tiled=True)
    psf, grad_u = intensity(field, psf_grad, clen, plen)
    gathered = lax.all_gather(grad_u, "ray", axis=0, tiled=True)
    partial_value = ray_partials(row_tab, col_tab, rows_x, all_cols, gathered)
    sums = lax.psum(partial_value, "pix")
    return (psf, finish(sums, rays))


def solution(mesh):
    in_specs = (P(None, "ray"), P(None, "ray"), P("ray"), P("ray"), P(None, "pix", "ray"))
    out_specs = (P(None, "pix", "ray"), P(None, "ray"))
    return jax.shard_map(
        on_device, mesh=mesh, in_specs=in_specs, out_specs=out_specs, check_vma=False
    )
```

profile of v0, /device:TPU:32, one launch (start us, length us, event | category | flops | bytes accessed | tf_op | source)
XLA Modules:
  0.0 497.8 jit_solution(16539537502296417018)
XLA Ops:
  9.5 3.6 cosine_multiply_fusion.2
  13.2 46.6 %multiply_cosine_fusion.2 = (f32[1,1024,1024]{2,1,0:T(8,128)}, f32[1,1024,1024]{2,1,0:T(8,128)}, f32[1,1024,1024]{2,1,0:T(8,128)}, f32[1,1024,1024]{2,1,0:T(8,12...) fusion(f32[1024]{0:T(1024)S(1)} %bitcast.214, f32[1024]{0:T(1024)S(1)} %fusion.111, ...), kind=kLoop, calls=%fused_computation.186 | loop fusion | flops 3145728 | bytes 25182208 | tf_op jit(solution)/shard_map/cos | solution.py:32
  62.8 9.3 %maximum_bitcast_fusion.1 = (f32[1,2,1024,1024]{3,2,1,0:T(8,128)S(1)}, f32[1,2,1024,1024]{3,2,1,0:T(8,128)}) fusion(f32[1,1024,1024]{2,1,0:T(8,128)} %get-tuple-element.336, f32[1,1024,1024]{2,1,0:T(8,128)} %get-tuple-element.335, f32[1,1024,1024]{2,1,0:T(8,128)} %get-tuple-element.341, f32[1,1024,1024]{2,1,0:T(8,128)} %get-tuple-element.342), kind=kLoop, calls=%fused_computation.178 | loop fusion | flops 4194304 | bytes 33554432 | tf_op jit(solution)/shard_map/stack | solution.py:33
  72.1 15.7 %fusion.115 = (bf16[3,2,1024,1024]{3,2,1,0:T(8,128)(2,1)}, f32[3,2,1024,1024]{3,2,1,0:T(8,128)}) fusion(f32[1,2,1024,1024]{3,2,1,0:T(8,128)S(1)} %maximum_bitcast_fusion.3, f32[1,2,1024,1024]{3,2,1,0:T(8,128)} %get-tuple-element.346, f32[1,2,1024,1024]{3,2,1,0:T(8,128)S(1)} %get-tuple-element.345), kind=kLoop, calls=%fused_computation.219 | loop fusion | flops 18874368 | bytes 62914560
  87.8 56.3 %while.27 = (s32[]{:T(128)}, f32[1024,384]{0,1:T(8,128)S(1)}, bf16[3,2,1024,1024]{3,2,1,0:T(8,128)(2,1)}, f32[3,2,1024,64]{2,3,1,0:T(8,128)}, s32[]{:T(128)}, /*...) while((s32[]{:T(128)}, f32[1024,384]{0,1:T(8,128)S(1)}, bf16[3,2,1024,1024]{3,2,1,0:T(8,128)(2,1)}, ...), condition=%wide.region_1.0_spmd.clone, body=%wide.region_0.0_spmd.clone.sunk | while | flops 412237824 | bytes 23888080 | solution.py:67
  96.0 2.5 fusion.173
  110.1 2.5 fusion.173
  124.2 2.5 fusion.173
  138.2 2.5 fusion.173
  145.9 87.3 %reduce-scatter.4.cloned.1.call-done = f32[64,384]{1,0:T(8,128)} async-done(((f32[1024,384]{1,0:T(8,128)}), f32[64,384]{1,0:T(8,128)}) %reduce-scatter.4.cloned.1.call-update) | async-done | bytes 98320
  234.4 51.1 %all_gather.3 = bf16[1024,384]{1,0:T(8,128)(2,1)} all-gather(bf16[64,384]{1,0:T(8,128)(2,1)S(1)} %copy.31), channel_id=1, replica_groups=mesh['ray'=16,'pix'=16] {'ray'}, dimensions={0}, use_global_device_ids=true | all-gather | bytes 835584 | tf_op jit(solution)/shard_map/all_gather | solution.py:140
  285.5 118.7 %while.26 = (s32[]{:T(128)}, f32[4,4,256]{2,1,0:T(4,128)S(1)}, s32[4]{0:T(128)S(1)}, f32[3,2,1024,1024]{3,2,1,0:T(8,128)}, bf16[1024,384]{1,0:T(8,128)(2,1)}, /*...) while((s32[]{:T(128)}, f32[4,4,256]{2,1,0:T(4,128)S(1)}, ...), condition=%wide.region_16.17_spmd.clone.clone, body=%wide.region_3.16_spmd.clone.clone.sunk | while | flops 819468480 | bytes 79344528 | solution.py:104
  286.7 5.2 %constant_dynamic-slice_fusion.15 = (f32[1,1,1024,256]{3,2,1,0:T(8,128)S(1)}, f32[1,1,1024,256]{3,2,1,0:T(8,128)}, f32[1,1,1024,256]{3,2,1,0:T(8,128)}, f32[1,1,...) fusion(f32[3,2,1024,1024]{3,2,1,0:T(8,128)} %get-tuple-element.584, ...), kind=kLoop, calls=%fused_computation.102.clone.1 | loop fusion | bytes 12582924 | tf_op jit(solution)/shard_map/while/body/eval_jaxpr/slice | solution.py:87
  295.7 2.5 copy.70
  304.3 2.5 copy.68
  316.4 5.2 %constant_dynamic-slice_fusion.15 = (f32[1,1,1024,256]{3,2,1,0:T(8,128)S(1)}, f32[1,1,1024,256]{3,2,1,0:T(8,128)}, f32[1,1,1024,256]{3,2,1,0:T(8,128)}, f32[1,1,...) fusion(f32[3,2,1024,1024]{3,2,1,0:T(8,128)} %get-tuple-element.584, ...), kind=kLoop, calls=%fused_computation.102.clone.1 | loop fusion | bytes 12582924 | tf_op jit(solution)/shard_map/while/body/eval_jaxpr/slice | solution.py:87
  325.4 2.5 copy.70
  334.0 2.5 copy.68
  346.1 5.2 %constant_dynamic-slice_fusion.15 = (f32[1,1,1024,256]{3,2,1,0:T(8,128)S(1)}, f32[1,1,1024,256]{3,2,1,0:T(8,128)}, f32[1,1,1024,256]{3,2,1,0:T(8,128)}, f32[1,1,...) fusion(f32[3,2,1024,1024]{3,2,1,0:T(8,128)} %get-tuple-element.584, ...), kind=kLoop, calls=%fused_computation.102.clone.1 | loop fusion | bytes 12582924 | tf_op jit(solution)/shard_map/while/body/eval_jaxpr/slice | solution.py:87
  355.1 2.5 copy.70
  363.7 2.5 copy.68
  375.8 5.2 %constant_dynamic-slice_fusion.15 = (f32[1,1,1024,256]{3,2,1,0:T(8,128)S(1)}, f32[1,1,1024,256]{3,2,1,0:T(8,128)}, f32[1,1,1024,256]{3,2,1,0:T(8,128)}, f32[1,1,...) fusion(f32[3,2,1024,1024]{3,2,1,0:T(8,128)} %get-tuple-element.584, ...), kind=kLoop, calls=%fused_computation.102.clone.1 | loop fusion | bytes 12582924 | tf_op jit(solution)/shard_map/while/body/eval_jaxpr/slice | solution.py:87
  393.3 2.5 copy.68
  404.2 84.1 %psum.7 = f32[4,1024]{1,0:T(4,128)S(1)} all-reduce(f32[4,1024]{1,0:T(4,128)S(1)} %bitcast.219), channel_id=1, replica_groups=mesh['ray'=16,'pix'=16] {'pix'}, use_global_device_ids=true, to_apply=%region_17.18 | all-reduce | flops 4096 | bytes 32768 | tf_op jit(solution)/shard_map/psum | solution.py:142
  (249 shorter events, 133.7 us)
Async XLA Ops:
  7.2 226.1 %reduce-scatter.4.cloned.1.call-start = ((), (), s32[]{:S(2)}) async-start(), calls=%async_computation.1 | async-start | bytes 1671168
  144.2 1.8 copy-start.6
  234.3 51.2 %copy-start.5 = (f32[64,384]{0,1:T(8,128)}, f32[64,384]{0,1:T(8,128)S(1)}, u32[]{:S(2)}) copy-start(f32[64,384]{0,1:T(8,128)S(1)} %copy.38) | copy-start | bytes 294916
  285.5 202.9 %copy-start.7 = (f32[2,1024]{1,0:T(2,128)S(1)}, f32[2,1024]{1,0:T(2,128)}, u32[]{:S(2)}) copy-start(f32[2,1024]{1,0:T(2,128)} %param.10) | copy-start | bytes 24580
  285.5 202.9 %copy-start.8 = (f32[2,1024]{1,0:T(2,128)S(1)}, f32[2,1024]{1,0:T(2,128)}, u32[]{:S(2)}) copy-start(f32[2,1024]{1,0:T(2,128)} %param.9) | copy-start | bytes 24580
  285.5 202.9 %copy-start.9 = (f32[1024]{0:T(1024)S(1)}, f32[1024]{0:T(1024)}, u32[]{:S(2)}) copy-start(f32[1024]{0:T(1024)} %param.12) | copy-start | bytes 12292
  306.8 1.8 copy-start.3
  306.8 2.3 copy-start.4
  311.4 1.4 copy-start
  311.4 1.5 copy-start.1
  311.4 1.8 copy-start.2
  336.5 1.8 copy-start.3
  336.5 2.3 copy-start.4
  341.1 1.5 copy-start.1
  341.1 1.8 copy-start.2
  366.2 1.8 copy-start.3
  366.2 2.3 copy-start.4
  370.8 1.4 copy-start
  370.8 1.5 copy-start.1
  370.8 1.8 copy-start.2
  395.9 1.8 copy-start.3
  395.9 2.3 copy-start.4
  400.4 1.5 copy-start.1
  400.5 1.8 copy-start.2
  (2 other events, 2.8 us)
Sparse Core Ops, SparseCore 0:
  146.0 87.1 reduce-scatter.3
where the time goes:
time: 501 us; the launch traced here: 498 us
  blocking collectives  135 us (27%)
  other arithmetic  114 us (23%)
  local copies, waits for them, and re-layouts  98.7 us (20%)
  waiting for transfers between devices  87.3 us (17%)
  matrix products  44.4 us (9%)
  between operations  14.2 us (3%)
    unnamed x2, waiting for transfers between devices  87.3 us
    psum x1, blocking collectives, on_device(): sums = lax.psum(partial_value, 'pix')  84.1 us
    all_gather x1, blocking collectives, on_device(): gathered = lax.all_gather(grad_u, 'ray', axis=0, tiled=True)  51.1 us
    cos x1, other arithmetic, build_tables(): col_list.append(jnp.stack([jnp.cos(beta), jnp.sin(beta)]))  46.6 us
    dot_general x36, matrix products, product(): lax.dot_general(left, right, dims, preferred_element_type=jnp.float32)  44.4 us
    while x88, local copies, waits for them, and re-layouts  43.5 us
    slice x4, local copies, waits for them, and re-layouts, one_block(): b_re = b_blk[wave, 0]  20.6 us
    another operation x24, other arithmetic  16 us
  transfers between devices with their start and end apart: 1, of which 1 were waited for; matrix products, arithmetic and copies ran while one was open for 0% of the time, Pallas kernels for 0%

commit v1 on v0

--- a/solution.py
+++ b/solution.py
@@ -7,6 +7,11 @@
 NPIX = 1024
 wave_scales = (1.2088, 1.0, 0.8953)
 two_pi = 2.0 * math.pi
+
+
+def gather_over(shard, mesh_axis, dim):
+    outgoing = jnp.stack([shard] * lax.axis_size(mesh_axis))
+    return jnp.concatenate(lax.all_to_all(outgoing, mesh_axis, 0, 0), axis=dim)
 
 
 def centred(start, count):
@@ -137,7 +142,7 @@
     row_tab, col_tab = build_tables(rays, rows_x, all_cols, norm)
     field = lax.psum_scatter(field_terms(row_tab, col_tab), "ray", scatter_dimension=0, tiled=True)
     psf, grad_u = intensity(field, psf_grad, clen, plen)
-    gathered = lax.all_gather(grad_u, "ray", axis=0, tiled=True)
+    gathered = gather_over(grad_u, "ray", 0)
     partial_value = ray_partials(row_tab, col_tab, rows_x, all_cols, gathered)
     sums = lax.psum(partial_value, "pix")
     return (psf, finish(sums, rays))

time: 501 us -> 486 us (0.970)
  blocking collectives: 135 us -> 84.1 us
  matrix products: 44.4 us -> 60.3 us
  waiting for transfers between devices: 87.3 us -> 98.7 us
  starting transfers between devices: 0.04 us -> 9.38 us
    all_gather x1 -> x0, blocking collectives: 51.1 us -> none  [on_device(): gathered = lax.all_gather(grad_u, 'ray', axis=0, tiled=True)]
    dot_general x36, matrix products: 44.4 us -> 60.3 us  [product(): lax.dot_general(left, right, dims, preferred_element_type=jnp.float32)]
    all_to_all x0 -> x1, waiting for transfers between devices: none -> 11.8 us  [gather_over(): return jnp.concatenate(lax.all_to_all(outgoing, mesh_axis, 0, 0), axis=dim)]
    all_to_all x0 -> x1, starting transfers between devices: none -> 9.34 us  [gather_over(): return jnp.concatenate(lax.all_to_all(outgoing, mesh_axis, 0, 0), axis=dim)]
    while x88 -> x80, local copies, waits for them, and re-layouts: 43.5 us -> 41.8 us
    another operation x8 -> x9, local copies, waits for them, and re-layouts: 12.5 us -> 13.6 us
  transfers between devices with their start and end apart: 1 -> 2, of which waited for: 1 -> 2; matrix products, arithmetic and copies ran while one was open for 0% -> 0% of each run, Pallas kernels for 0% -> 0%
where the time goes in v1:
time: 486 us; the launch traced here: 482 us
  other arithmetic  114 us (23%)
  waiting for transfers between devices  98.7 us (20%)
  local copies, waits for them, and re-layouts  97.1 us (20%)
  blocking collectives  84.1 us (17%)
  matrix products  60.3 us (12%)
  between operations  14.2 us (3%)
  starting transfers between devices  9.38 us (2%)
    unnamed x2, waiting for transfers between devices  86.9 us
    psum x1, blocking collectives, on_device(): sums = lax.psum(partial_value, 'pix')  84.1 us
    dot_general x36, matrix products, product(): lax.dot_general(left, right, dims, preferred_element_type=jnp.float32)  60.3 us
    cos x1, other arithmetic, build_tables(): col_list.append(jnp.stack([jnp.cos(beta), jnp.sin(beta)]))  46.6 us
    while x80, local copies, waits for them, and re-layouts  41.8 us
    slice x4, local copies, waits for them, and re-layouts, one_block(): b_re = b_blk[wave, 0]  20.6 us
    another operation x24, other arithmetic  15.8 us
    unnamed x2, other arithmetic  15.7 us
  transfers between devices with their start and end apart: 2, of which 2 were waited for; matrix products, arithmetic and copies ran while one was open for 0% of the time, Pallas kernels for 0%

profile of v1, /device:TPU:32, one launch (start us, length us, event | category | flops | bytes accessed | tf_op | source)
XLA Modules:
  0.0 481.6 jit_solution(7906310572180617692)
XLA Ops:
  9.5 3.6 cosine_multiply_fusion.2
  13.2 46.6 %multiply_cosine_fusion.2 = (f32[1,1024,1024]{2,1,0:T(8,128)}, f32[1,1024,1024]{2,1,0:T(8,128)}, f32[1,1024,1024]{2,1,0:T(8,128)}, f32[1,1024,1024]{2,1,0:T(8,12...) fusion(f32[1024]{0:T(1024)S(1)} %bitcast.215, f32[1024]{0:T(1024)S(1)} %fusion.111, ...), kind=kLoop, calls=%fused_computation.186 | loop fusion | flops 3145728 | bytes 25182208 | tf_op jit(solution)/shard_map/cos | solution.py:37
  62.8 9.3 %maximum_bitcast_fusion.1 = (f32[1,2,1024,1024]{3,2,1,0:T(8,128)S(1)}, f32[1,2,1024,1024]{3,2,1,0:T(8,128)}) fusion(f32[1,1024,1024]{2,1,0:T(8,128)} %get-tuple-element.336, f32[1,1024,1024]{2,1,0:T(8,128)} %get-tuple-element.335, f32[1,1024,1024]{2,1,0:T(8,128)} %get-tuple-element.341, f32[1,1024,1024]{2,1,0:T(8,128)} %get-tuple-element.342), kind=kLoop, calls=%fused_computation.178 | loop fusion | flops 4194304 | bytes 33554432 | tf_op jit(solution)/shard_map/stack | solution.py:38
  72.1 15.7 %fusion.115 = (bf16[3,2,1024,1024]{3,2,1,0:T(8,128)(2,1)}, f32[3,2,1024,1024]{3,2,1,0:T(8,128)}) fusion(f32[1,2,1024,1024]{3,2,1,0:T(8,128)S(1)} %maximum_bitcast_fusion.3, f32[1,2,1024,1024]{3,2,1,0:T(8,128)} %get-tuple-element.346, f32[1,2,1024,1024]{3,2,1,0:T(8,128)S(1)} %get-tuple-element.345), kind=kLoop, calls=%fused_computation.219 | loop fusion | flops 18874368 | bytes 62914560
  87.8 56.3 %while.27 = (s32[]{:T(128)}, f32[1024,384]{0,1:T(8,128)S(1)}, bf16[3,2,1024,1024]{3,2,1,0:T(8,128)(2,1)}, f32[3,2,1024,64]{2,3,1,0:T(8,128)}, s32[]{:T(128)}, /*...) while((s32[]{:T(128)}, f32[1024,384]{0,1:T(8,128)S(1)}, bf16[3,2,1024,1024]{3,2,1,0:T(8,128)(2,1)}, ...), condition=%wide.region_1.0_spmd.clone, body=%wide.region_0.0_spmd.clone.sunk | while | flops 412237824 | bytes 23888080 | solution.py:72
  96.0 2.5 fusion.173
  110.1 2.5 fusion.173
  124.2 2.5 fusion.173
  138.2 2.5 fusion.173
  145.9 86.9 %reduce-scatter.4.cloned.1.call-done = f32[64,384]{1,0:T(8,128)} async-done(((f32[1024,384]{1,0:T(8,128)}), f32[64,384]{1,0:T(8,128)}) %reduce-scatter.4.cloned.1.call-update) | async-done | bytes 98320
  235.0 9.3 %all-to-all-start = ((bf16[16,64,384]{2,1,0:T(8,128)(2,1)}), bf16[16,64,384]{2,1,0:T(8,128)(2,1)}, u32[]{:S(2)}, u32[]{:S(2)}) async-start(bf16[16,64,384]{2,1,0:T(8,128)(2,1)} %stack.55), calls=%async_computation | async-start | bytes 1572864 | tf_op jit(solution)/shard_map/all_to_all | solution.py:14
  245.4 11.8 %all-to-all-done = bf16[16,64,384]{2,1,0:T(8,128)(2,1)} async-done(((bf16[16,64,384]{2,1,0:T(8,128)(2,1)}), bf16[16,64,384]{2,1,0:T(8,128)(2,1)}, u32[]{:S(2)}, u32[]{:S(2)}) %all-to-all-start) | async-done | bytes 786464 | tf_op jit(solution)/shard_map/all_to_all | solution.py:14
  257.2 132.7 %while.26 = (s32[]{:T(128)}, f32[4,4,256]{2,1,0:T(4,128)S(1)}, s32[4]{0:T(128)S(1)}, f32[3,2,1024,1024]{3,2,1,0:T(8,128)}, bf16[1024,384]{1,0:T(8,128)(2,1)}, /*...) while((s32[]{:T(128)}, f32[4,4,256]{2,1,0:T(4,128)S(1)}, ...), condition=%wide.region_16.17_spmd.clone.clone, body=%wide.region_3.16_spmd.clone.clone.sunk | while | flops 819468480 | bytes 76198768 | solution.py:109
  258.4 5.2 %constant_dynamic-slice_fusion.15 = (f32[1,1,1024,256]{3,2,1,0:T(8,128)S(1)}, f32[1,1,1024,256]{3,2,1,0:T(8,128)}, f32[1,1,1024,256]{3,2,1,0:T(8,128)}, f32[1,1,...) fusion(f32[3,2,1024,1024]{3,2,1,0:T(8,128)} %get-tuple-element.584, ...), kind=kLoop, calls=%fused_computation.102.clone.1 | loop fusion | bytes 12582924 | tf_op jit(solution)/shard_map/while/body/eval_jaxpr/slice | solution.py:92
  267.4 2.5 copy.70
  276.0 2.5 copy.68
  291.6 5.2 %constant_dynamic-slice_fusion.15 = (f32[1,1,1024,256]{3,2,1,0:T(8,128)S(1)}, f32[1,1,1024,256]{3,2,1,0:T(8,128)}, f32[1,1,1024,256]{3,2,1,0:T(8,128)}, f32[1,1,...) fusion(f32[3,2,1024,1024]{3,2,1,0:T(8,128)} %get-tuple-element.584, ...), kind=kLoop, calls=%fused_computation.102.clone.1 | loop fusion | bytes 12582924 | tf_op jit(solution)/shard_map/while/body/eval_jaxpr/slice | solution.py:92
  300.6 2.5 copy.70
  309.2 2.5 copy.68
  324.8 5.2 %constant_dynamic-slice_fusion.15 = (f32[1,1,1024,256]{3,2,1,0:T(8,128)S(1)}, f32[1,1,1024,256]{3,2,1,0:T(8,128)}, f32[1,1,1024,256]{3,2,1,0:T(8,128)}, f32[1,1,...) fusion(f32[3,2,1024,1024]{3,2,1,0:T(8,128)} %get-tuple-element.584, ...), kind=kLoop, calls=%fused_computation.102.clone.1 | loop fusion | bytes 12582924 | tf_op jit(solution)/shard_map/while/body/eval_jaxpr/slice | solution.py:92
  342.3 2.5 copy.68
  357.9 5.2 %constant_dynamic-slice_fusion.15 = (f32[1,1,1024,256]{3,2,1,0:T(8,128)S(1)}, f32[1,1,1024,256]{3,2,1,0:T(8,128)}, f32[1,1,1024,256]{3,2,1,0:T(8,128)}, f32[1,1,...) fusion(f32[3,2,1024,1024]{3,2,1,0:T(8,128)} %get-tuple-element.584, ...), kind=kLoop, calls=%fused_computation.102.clone.1 | loop fusion | bytes 12582924 | tf_op jit(solution)/shard_map/while/body/eval_jaxpr/slice | solution.py:92
  375.5 2.5 copy.68
  389.9 84.1 %psum.7 = f32[4,1024]{1,0:T(4,128)S(1)} all-reduce(f32[4,1024]{1,0:T(4,128)S(1)} %bitcast.220), channel_id=1, replica_groups=mesh['ray'=16,'pix'=16] {'pix'}, use_global_device_ids=true, to_apply=%region_17.18 | all-reduce | flops 4096 | bytes 32768 | tf_op jit(solution)/shard_map/psum | solution.py:147
  (241 shorter events, 150.4 us)
Async XLA Ops:
  7.2 225.7 %reduce-scatter.4.cloned.1.call-start = ((), (), s32[]{:S(2)}) async-start(), calls=%async_computation.2 | async-start | bytes 1671168
  144.2 1.7 copy-start.4
  235.0 22.1 %all-to-all-start = ((bf16[16,64,384]{2,1,0:T(8,128)(2,1)}), bf16[16,64,384]{2,1,0:T(8,128)(2,1)}, u32[]{:S(2)}, u32[]{:S(2)}) async-start(bf16[16,64,384]{2,1,0:T(8,128)(2,1)} %stack.55), calls=%async_computation | async-start | bytes 1572864 | tf_op jit(solution)/shard_map/all_to_all | solution.py:14
  257.2 216.8 %copy-start.5 = (f32[2,1024]{1,0:T(2,128)S(1)}, f32[2,1024]{1,0:T(2,128)}, u32[]{:S(2)}) copy-start(f32[2,1024]{1,0:T(2,128)} %param.10) | copy-start | bytes 24580
  257.2 216.8 %copy-start.6 = (f32[2,1024]{1,0:T(2,128)S(1)}, f32[2,1024]{1,0:T(2,128)}, u32[]{:S(2)}) copy-start(f32[2,1024]{1,0:T(2,128)} %param.9) | copy-start | bytes 24580
  257.2 216.9 %copy-start.7 = (f32[1024]{0:T(1024)S(1)}, f32[1024]{0:T(1024)}, u32[]{:S(2)}) copy-start(f32[1024]{0:T(1024)} %param.12) | copy-start | bytes 12292
  278.5 3.2 copy-start.3
  284.0 4.4 copy-start
  284.0 4.4 copy-start.1
  284.0 4.4 copy-start.2
  311.7 3.2 copy-start.3
  317.2 4.4 copy-start
  317.2 4.4 copy-start.1
  317.2 4.4 copy-start.2
  344.9 3.2 copy-start.3
  350.3 4.4 copy-start
  350.4 4.4 copy-start.1
  350.4 4.4 copy-start.2
  378.0 3.2 copy-start.3
  383.5 4.4 copy-start
  383.5 4.4 copy-start.1
  383.5 4.4 copy-start.2
Sparse Core Ops, SparseCore 0:
  146.0 86.7 reduce-scatter.3
